TPU v7x, 128 devices: a whole 4x4x4 slice. The times are simulated.
128 devices in a mesh: bx: 16 (over x, z), by: 8 (over y, core).
Axes of the slice: x: 4, y: 4, z: 4, core: 2. Of those that a mesh axis runs over, the one named last changes fastest.
Arguments:
- features: bfloat16 [16, 8, 1024, 128], P('bx', 'by'), may hold values from -13 to 13
- live_count: int32 [16, 8], P('bx', 'by'), may hold values from 128 to 1024, as said below
- neighbour_map: int32 [16, 8, 27, 1024], P('bx', 'by'), may hold values from 0 to 2175, as said below
- send_rows: int32 [16, 8, 8, 128], P('bx', 'by'), may hold values from 0 to 1023, as said below
- weight: bfloat16 [3456, 128], replicated, may hold values from -0.109375 to 0.109375
- gain: float32 [128], replicated, may hold values from 0.5 to 1.5
- shift: float32 [128], replicated, may hold values from -3 to 3
- cotangent: bfloat16 [16, 8, 1024, 128], P('bx', 'by'), may hold values from -13 to 13
Outputs:
- activated: bfloat16 [16, 8, 1024, 128], P('bx', 'by')
- grad_features: bfloat16 [16, 8, 1024, 128], P('bx', 'by')
- grad_weight: float32 [27, 128, 128], P(None, 'bx', 'by')
Inputs may be any that keep to these rules, and one draw needn't show every extreme that they name: Rows 0 to live_count - 1 of a brick are live, the rest padding; in every draw some brick is full. `send_rows`: every entry is below its brick's live count; the eight blocks follow the directions (dx, dy) in row-major order with the brick's own position left out. `neighbour_map`: entries index the brick's extended table; offset 13 of a live row names that row itself; every entry of a padding row is 1536. With B = min(1024, 512) and q = r // B for a live row r, an entry below 1024 lies in rows q B to q B + B - 1, and an entry 1024 + b * 128 + h of incoming block b other than 4 has h in q * 128 B / 1024 to (q + 1) * 128 B / 1024 - 1.
All inputs are finite; a program needn't handle non-finite values.
Results may differ from a plain program's by a relative error of at most 0.029.
The roundings to bfloat16 on the way count: a program that leaves them out, or rounds other values in their place, can miss the bound.
Values may be sent and summed in bfloat16 or wider, within the bound.
No kernel may reach another device: no remote copies, remote signals or barrier semaphores. Data moves between devices by JAX's collectives and lax.ppermute only.
A program may use at most 64 MiB of HBM per device.

v0:
```python
import jax
import jax.numpy as jnp
from jax import lax
from jax.sharding import PartitionSpec as P

epsilon = 1e-05


def extended(cells, sides, width):
    for axis, dim in sides:
        count = lax.axis_size(axis)
        ends = count - 1
        head = lax.slice_in_dim(cells, 0, width, axis=dim)
        tail = lax.slice_in_dim(cells, cells.shape[dim] - width, cells.shape[dim], axis=dim)
        cells = jnp.concatenate(
            [
                lax.ppermute(tail, axis, [(i, (i + 1) % count) for i in range(ends)]),
                cells,
                lax.ppermute(head, axis, [((i + 1) % count, i) for i in range(ends)]),
            ],
            axis=dim,
        )
    return cells


def from_neighbours(outgoing):
    padded = extended(outgoing, (("bx", 0), ("by", 1)), 1)
    return padded[::2, ::2]


def per_device(features, live_count, neighbour_map, send_rows, weight, gain, shift, cotangent):
    own_rows = features[0, 0]
    rows_total, channels = own_rows.shape
    halo_rows = send_rows.shape[3]
    block_rows = min(rows_total, 512)
    blocks_count = rows_total // block_rows
    halo_window = halo_rows // blocks_count
    window_rows = block_rows + 9 * halo_window
    sent_index = send_rows[0, 0].reshape(-1)
    send_select = (
        sent_index[:, None] == lax.broadcasted_iota(jnp.int32, (1, rows_total), 1)
    ).astype(jnp.bfloat16)
    chosen_rows = jnp.dot(send_select, own_rows, preferred_element_type=jnp.float32).astype(
        jnp.bfloat16
    )
    chosen_rows = chosen_rows.reshape(8, halo_rows, channels)
    blank_block = jnp.zeros((1, halo_rows, channels), jnp.bfloat16)
    outgoing = jnp.concatenate([chosen_rows[:4], blank_block, chosen_rows[4:]], axis=0).reshape(
        3, 3, halo_rows, channels
    )
    incoming = from_neighbours(outgoing).reshape(9, blocks_count, halo_window, channels)
    index_blocks = neighbour_map[0, 0].reshape(27, blocks_count, block_rows).transpose(1, 0, 2)
    own_blocks = own_rows.reshape(blocks_count, block_rows, channels)
    halo_blocks = incoming.transpose(1, 0, 2, 3)
    block_ids = jnp.arange(blocks_count, dtype=jnp.int32)

    def selector_of(indices, block_index):
        beyond = indices - rows_total
        target = beyond // halo_rows
        inside = beyond - target * halo_rows - block_index * halo_window
        local_pos = indices - block_index * block_rows
        remote_pos = block_rows + target * halo_window + inside
        usable = (inside >= 0) & (inside < halo_window)
        position = jnp.where(indices < rows_total, local_pos, jnp.where(usable, remote_pos, -1))
        return position[:, :, None] == lax.broadcasted_iota(jnp.int32, (1, 1, window_rows), 2)

    def forward_block(pieces):
        indices, own_part, halo_part, block_index = pieces
        window = jnp.concatenate([own_part, halo_part.reshape(9 * halo_window, channels)], axis=0)
        selector = selector_of(indices, block_index).astype(jnp.bfloat16)
        gathered = jnp.einsum(
            "kbw,wc->bkc", selector, window, preferred_element_type=jnp.float32
        ).astype(jnp.bfloat16)
        columns = gathered.reshape(block_rows, 27 * channels)
        return (jnp.dot(columns, weight, preferred_element_type=jnp.float32), columns)

    conv_blocks, column_blocks = lax.map(
        forward_block, (index_blocks, own_blocks, halo_blocks, block_ids)
    )
    conv_out = conv_blocks.reshape(rows_total, channels).astype(jnp.bfloat16)
    conv_float = conv_out.astype(jnp.float32)
    live_mask = (lax.broadcasted_iota(jnp.int32, (rows_total, 1), 0) < live_count[0, 0]).astype(
        jnp.float32
    )
    local_count = jnp.sum(live_mask)
    total_sum, total_count = lax.psum(
        (jnp.sum(conv_float * live_mask, axis=0), local_count), ("bx", "by")
    )
    center = total_sum / total_count
    deviation = (conv_float - center) * live_mask
    variance = lax.psum(jnp.sum(deviation * deviation, axis=0), ("bx", "by")) / total_count
    inverse_std = lax.rsqrt(variance + epsilon)
    normalized = (conv_float - center) * inverse_std
    before = gain * normalized + shift
    activated = (jnp.maximum(before, 0.0) * live_mask).astype(jnp.bfloat16)
    upstream = cotangent[0, 0].astype(jnp.float32) * (before > 0.0) * live_mask
    sum_up, sum_cross = lax.psum(
        (jnp.sum(upstream, axis=0), jnp.sum(upstream * normalized, axis=0)), ("bx", "by")
    )
    conv_grad = (
        gain
        * inverse_std
        * (upstream - live_mask * (sum_up + normalized * sum_cross) / total_count)
    ).astype(jnp.bfloat16)
    grad_blocks = conv_grad.reshape(blocks_count, block_rows, channels)

    def backward_block(weight_acc, pieces):
        indices, columns, grad_rows, block_index = pieces
        weight_acc = weight_acc + lax.dot_general(
            columns, grad_rows, (((0,), (0,)), ((), ())), preferred_element_type=jnp.float32
        )
        column_grad = lax.dot_general(
            grad_rows, weight, (((1,), (1,)), ((), ())), preferred_element_type=jnp.float32
        )
        column_grad = column_grad.reshape(block_rows, 27, channels)
        selector = selector_of(indices, block_index).astype(jnp.float32)
        window_grad = jnp.einsum(
            "kbw,bkc->wc",
            selector,
            column_grad,
            precision=lax.Precision.HIGHEST,
            preferred_element_type=jnp.float32,
        )
        return (
            weight_acc,
            (window_grad[:block_rows], window_grad[block_rows:].reshape(9, halo_window, channels)),
        )

    start_acc = jnp.zeros((27 * channels, channels), jnp.float32)
    weight_acc, (own_parts, halo_parts) = lax.scan(
        backward_block, start_acc, (index_blocks, column_blocks, grad_blocks, block_ids)
    )
    weight_terms = weight_acc.reshape(27, channels, channels)
    partial_x = lax.psum_scatter(
        weight_terms.astype(jnp.bfloat16), "bx", scatter_dimension=1, tiled=True
    )
    summed = lax.psum_scatter(partial_x, "by", scatter_dimension=2, tiled=True).astype(jnp.float32)
    grad_weight = summed / jnp.sqrt(total_count)
    own_table = own_parts.reshape(rows_total, channels)
    halo_table = halo_parts.transpose(1, 0, 2, 3).reshape(3, 3, halo_rows, channels)
    halo_grad = halo_table.astype(jnp.bfloat16)
    returned = from_neighbours(halo_grad).reshape(9, halo_rows, channels)
    slots_back = (
        jnp.concatenate([returned[:4], returned[5:]], axis=0)
        .reshape(-1, channels)
        .astype(jnp.float32)
    )
    added_back = lax.dot_general(
        send_select.astype(jnp.float32),
        slots_back,
        (((0,), (0,)), ((), ())),
        precision=lax.Precision.HIGHEST,
        preferred_element_type=jnp.float32,
    )
    own_grad = own_table + added_back
    return (activated[None, None], own_grad.astype(jnp.bfloat16)[None, None], grad_weight)


def solution(mesh):
    return jax.shard_map(
        per_device,
        mesh=mesh,
        in_specs=(
            P("bx", "by", None, None),
            P("bx", "by"),
            P("bx", "by", None, None),
            P("bx", "by", None, None),
            P(),
            P(),
            P(),
            P("bx", "by", None, None),
        ),
        out_specs=(P("bx", "by", None, None), P("bx", "by", None, None), P(None, "bx", "by")),
        check_vma=False,
    )
```

profile of v0, /device:TPU:0, one launch (start us, length us, event | category | flops | bytes accessed | tf_op | source)
XLA Modules:
  0.0 465.1 jit_solution(409183118276341036)
XLA Ops:
  7.2 1.9 fusion.34
  9.1 3.9 collective-permute-start
  13.0 1.3 collective-permute-start.1
  15.2 4.3 collective-permute-done.1
  20.3 1.9 collective-permute-start.2
  22.2 1.3 collective-permute-start.3
  25.5 1.5 collective-permute-done.3
  28.2 38.2 %while.33 = (s32[]{:T(128)}, bf16[2,512,128]{2,1,0:T(8,128)(2,1)S(1)}, bf16[2,512,3456]{1,2,0:T(8,128)(2,1)}, bf16[2,512,128]{2,1,0:T(8,128)(2,1)}, bf16[2,9,64,...) while((s32[]{:T(128)}, ...), condition=%wide.region_1.2_spmd.clone, body=%wide.region_0.1_spmd.sunk.clone | while | flops 4321123840 | bytes 16304801 | solution.py:77
  31.2 13.0 %fusion.82 = bf16[128,27,512]{2,0,1:T(8,128)(2,1)S(1)} fusion(s32[27,512]{1,0:T(8,128)S(1)} %bitcast_select_fusion.6, bf16[576,128]{1,0:T(8,128)(2,1)S(1)} %bitcast.223, bf16[512,128]{1,0:T(8,128)(2,1)S(1)} %dynamic-slice_bitcast_fusion.3), kind=kOutput, calls=%fused_computation.3.clone.1.clone | convolution fusion | flops 3867738112 | bytes 3872768 | tf_op jit(solution)/shard_map/while/body/eval_jaxpr/kbw,wc->bkc/dot_general | solution.py:71
  44.1 2.0 constant_dynamic-update-slice_fusion.6
  46.1 1.2 fusion.83
  50.2 13.0 %fusion.82 = bf16[128,27,512]{2,0,1:T(8,128)(2,1)S(1)} fusion(s32[27,512]{1,0:T(8,128)S(1)} %bitcast_select_fusion.6, bf16[576,128]{1,0:T(8,128)(2,1)S(1)} %bitcast.223, bf16[512,128]{1,0:T(8,128)(2,1)S(1)} %dynamic-slice_bitcast_fusion.3), kind=kOutput, calls=%fused_computation.3.clone.1.clone | convolution fusion | flops 3867738112 | bytes 3872768 | tf_op jit(solution)/shard_map/while/body/eval_jaxpr/kbw,wc->bkc/dot_general | solution.py:71
  63.2 2.0 constant_dynamic-update-slice_fusion.6
  66.6 70.3 %all-reduce.2 = (f32[128]{0:T(128)S(1)}, f32[]{:T(128)}) all-reduce(f32[128]{0:T(128)S(1)} %multiply_reduce_fusion.1, f32[]{:T(128)} %fusion.44), channel_id=1, replica_groups=mesh['bx'=16,'by'=8] {'bx','by'}, use_global_device_ids=true, to_apply=%region_3.4 | all-reduce | flops 129 | bytes 1032 | tf_op jit(solution)/shard_map/psum | solution.py:86
  137.8 62.7 %psum.37 = f32[128]{0:T(128)S(1)} all-reduce(f32[128]{0:T(128)S(1)} %multiply_reduce_fusion), channel_id=1, replica_groups=mesh['bx'=16,'by'=8] {'bx','by'}, use_global_device_ids=true, to_apply=%region_7.8 | all-reduce | flops 128 | bytes 1024 | tf_op jit(solution)/shard_map/psum | solution.py:91
  201.2 1.2 fusion.39
  202.4 64.2 %all-reduce.1 = (f32[128]{0:T(128)S(1)}, f32[128]{0:T(128)S(1)}) all-reduce(f32[128]{0:T(128)S(1)} %get-tuple-element.329, f32[128]{0:T(128)S(1)} %get-tuple-element.328), channel_id=1, replica_groups=mesh['bx'=16,'by'=8] {'bx','by'}, use_global_device_ids=true, to_apply=%region_11.12 | all-reduce | flops 256 | bytes 2048 | tf_op jit(solution)/shard_map/psum | solution.py:97
  266.6 1.9 fusion.42
  268.5 73.1 %while.34 = (s32[]{:T(128)}, f32[3456,128]{1,0:T(8,128)S(1)}, f32[2,512,128]{2,1,0:T(8,128)}, bf16[2,9,64,128]{3,2,0,1:T(8,128)(2,1)}, bf16[2,512,3456]{1,2,0:T(...) while((s32[]{:T(128)}, f32[3456,128]{1,0:T(8,128)S(1)}, ...), condition=%wide.region_13.14_spmd.clone.clone, body=%wide.region_12.13_spmd.clone.sunk.clone | while | flops 24024522752 | bytes 28413672 | solution.py:130
  271.6 28.7 %fusion.90 = f32[1088,128]{1,0:T(8,128)S(1)} fusion(f32[512,27,128]{2,0,1:T(8,128)S(1)} %fusion.89, s32[27,512]{1,0:T(8,128)S(1)} %bitcast_select_fusion.7), kind=kOutput, calls=%fused_computation.31.clone.1.clone | convolution fusion | flops 23117266944 | bytes 7690240 | tf_op jit(solution)/shard_map/while/body/eval_jaxpr/kbw,bkc->wc/dot_general | solution.py:117
  301.8 3.2 convolution_add_fusion.3
  308.2 28.7 %fusion.90 = f32[1088,128]{1,0:T(8,128)S(1)} fusion(f32[512,27,128]{2,0,1:T(8,128)S(1)} %fusion.89, s32[27,512]{1,0:T(8,128)S(1)} %bitcast_select_fusion.7), kind=kOutput, calls=%fused_computation.31.clone.1.clone | convolution fusion | flops 23117266944 | bytes 7690240 | tf_op jit(solution)/shard_map/while/body/eval_jaxpr/kbw,bkc->wc/dot_general | solution.py:117
  338.4 3.2 convolution_add_fusion.3
  343.7 1.3 collective-permute-start.4
  345.0 1.3 collective-permute-start.5
  348.3 4.0 collective-permute-done.5
  353.3 1.5 collective-permute-start.6
  354.8 1.3 collective-permute-start.7
  357.1 2.2 collective-permute-done.7
  360.5 64.4 %all-reduce.5.cloned.1.call-done = bf16[27,128,128]{2,1,0:T(8,128)(2,1)} async-done(((bf16[27,128,128]{2,1,0:T(8,128)(2,1)}), bf16[27,128,128]{2,1,0:T(8,128)(2,1)}) %all-reduce.5.cloned.1.call-update) | async-done | bytes 884752
  426.7 3.2 fusion.35
  429.9 27.0 %reduce-scatter.3.cloned.1.call-done = bf16[27,8,16]{0,1,2:T(8,128)(2,1)} async-done(((bf16[27,8,128]{0,1,2:T(8,128)(2,1)}), bf16[27,8,16]{0,1,2:T(8,128)(2,1)}) %reduce-scatter.3.cloned.1.call-update) | async-done | bytes 6928 | tf_op jit(solution)/shard_map/reduce_scatter | solution.py:137
  (84 shorter events, 25.5 us)
Async XLA Ops:
  7.2 21.0 %copy-start = (bf16[3456,128]{1,0:T(8,128)(2,1)S(1)}, bf16[3456,128]{1,0:T(8,128)(2,1)}, u32[]{:S(2)}) copy-start(bf16[3456,128]{1,0:T(8,128)(2,1)} %param.16) | copy-start | bytes 2654212
  7.2 417.8 %all-reduce.5.cloned.1.call-start = ((), (), s32[]{:S(2)}) async-start(), calls=%async_computation.2 | async-start | bytes 1769472
  9.1 6.1 %collective-permute-start = (bf16[1,3,128,128]{3,2,1,0:T(8,128)(2,1)S(1)}, bf16[1,3,128,128]{3,2,1,0:T(8,128)(2,1)S(1)}, u32[]{:S(2)}, u32[]{:S(2)}) collective-permute-start(bf16[1,3,128,128]{3,2,1,0:T(8,128)(2,1)S(1)} %bitcast.239), channel_id=1, source_target_pairs={{0,8},{8,16},{16,24},{24,32},{32,40},{40,48},{48,56},{56,64},{64,7... | collective-permute-start | bytes 294920 | tf_op jit(solution)/shard_map/ppermute | solution.py:17
  13.0 6.5 %collective-permute-start.1 = (bf16[1,3,128,128]{3,2,1,0:T(8,128)(2,1)S(1)}, bf16[1,3,128,128]{3,2,1,0:T(8,128)(2,1)S(1)}, u32[]{:S(2)}, u32[]{:S(2)}) collective-permute-start(bf16[1,3,128,128]{3,2,1,0:T(8,128)(2,1)S(1)} %bitcast.238), channel_id=1, source_target_pairs={{8,0},{16,8},{24,16},{32,24},{40,32},{48,40},{56,48},{64,56},{72,6... | collective-permute-start | bytes 294920 | tf_op jit(solution)/shard_map/ppermute | solution.py:19
  20.3 5.2 %collective-permute-start.2 = (bf16[5,1,128,128]{3,2,1,0:T(8,128)(2,1)}, bf16[5,1,128,128]{3,2,1,0:T(8,128)(2,1)}, u32[]{:S(2)}, u32[]{:S(2)}) collective-permute-start(bf16[5,1,128,128]{3,2,1,0:T(8,128)(2,1)} %get-tuple-element.372), channel_id=1, source_target_pairs={{0,1},{1,2},{2,3},{3,4},{4,5},{5,6},{6,7},{8,9},{9,10},{10,11},{11... | collective-permute-start | bytes 491528 | tf_op jit(solution)/shard_map/ppermute | solution.py:17
  22.2 4.8 %collective-permute-start.3 = (bf16[5,1,128,128]{3,2,1,0:T(8,128)(2,1)}, bf16[5,1,128,128]{3,2,1,0:T(8,128)(2,1)}, u32[]{:S(2)}, u32[]{:S(2)}) collective-permute-start(bf16[5,1,128,128]{3,2,1,0:T(8,128)(2,1)} %get-tuple-element.373), channel_id=1, source_target_pairs={{1,0},{2,1},{3,2},{4,3},{5,4},{6,5},{7,6},{9,8},{10,9},{11,10},{12... | collective-permute-start | bytes 491528 | tf_op jit(solution)/shard_map/ppermute | solution.py:19
  28.2 172.3 %copy-start.1 = (f32[128]{0:T(128)S(1)}, f32[128]{0:T(128)}, u32[]{:S(2)}) copy-start(f32[128]{0:T(128)} %param.17) | copy-start | bytes 1540
  28.2 173.0 %copy-start.2 = (f32[128]{0:T(128)S(1)}, f32[128]{0:T(128)}, u32[]{:S(2)}) copy-start(f32[128]{0:T(128)} %param.18) | copy-start | bytes 1540
  268.5 77.9 %copy-start.6 = (u32[128]{0:T(128)S(1)}, u32[128]{0:T(128)}, u32[]{:S(2)}) copy-start(u32[128]{0:T(128)} %constant.182) | copy-start | bytes 1540
  271.6 28.7 %copy-start.3 = (f32[2,512,128]{2,1,0:T(8,128)S(1)}, f32[2,512,128]{2,1,0:T(8,128)}, u32[]{:S(2)}) copy-start(f32[2,512,128]{2,1,0:T(8,128)} %get-tuple-element.580) | copy-start | bytes 1572868 | tf_op jit(solution)/shard_map/while
  300.4 0.8 copy-start.4
  308.1 28.7 %copy-start.3 = (f32[2,512,128]{2,1,0:T(8,128)S(1)}, f32[2,512,128]{2,1,0:T(8,128)}, u32[]{:S(2)}) copy-start(f32[2,512,128]{2,1,0:T(8,128)} %get-tuple-element.580) | copy-start | bytes 1572868 | tf_op jit(solution)/shard_map/while
  336.9 0.8 copy-start.4
  341.6 85.0 %copy-start.5 = (s32[1,1,8,128]{3,2,1,0:T(8,128)S(1)}, s32[1,1,8,128]{3,2,1,0:T(8,128)}, u32[]{:S(2)}) copy-start(s32[1,1,8,128]{3,2,1,0:T(8,128)} %param.15) | copy-start | bytes 12292
  342.7 114.2 %reduce-scatter.3.cloned.1.call-start = ((), (), s32[]{:S(2)}) async-start(), calls=%async_computation.1 | async-start | bytes 294912 | tf_op jit(solution)/shard_map/reduce_scatter | solution.py:137
  343.7 4.6 collective-permute-start.4
  345.0 7.3 %collective-permute-start.5 = (bf16[1,3,128,128]{3,2,1,0:T(8,128)(2,1)S(1)}, bf16[1,3,128,128]{3,2,1,0:T(8,128)(2,1)S(1)}, u32[]{:S(2)}, u32[]{:S(2)}) collective-permute-start(bf16[1,3,128,128]{3,2,1,0:T(8,128)(2,1)S(1)} %bitcast.236), channel_id=1, source_target_pairs={{8,0},{16,8},{24,16},{32,24},{40,32},{48,40},{56,48},{64,56},{72,6... | collective-permute-start | bytes 294920 | tf_op jit(solution)/shard_map/ppermute | solution.py:19
  353.3 3.7 collective-permute-start.6
  354.8 4.5 collective-permute-start.7
Sparse Core Ops, SparseCore 0:
  342.8 82.0 all-reduce.4
  427.3 29.5 reduce-scatter.2
where the time goes:
time: 466 us; the launch traced here: 465 us
  blocking collectives  197 us (42%)
  waiting for transfers between devices  104 us (22%)
  matrix products  99.4 us (21%)
  between operations  16.4 us (4%)
  local copies, waits for them, and re-layouts  15.4 us (3%)
  starting transfers between devices  13.9 us (3%)
  other arithmetic  13.7 us (3%)
  loops' own time  5.44 us (1%)
    psum x1, blocking collectives, per_device(): lax.psum((jnp.sum(conv_float * live_mask, axis=0), local_count), ('bx', '...  70.3 us
    unnamed x3, waiting for transfers between devices  64.5 us
    psum x1, blocking collectives, per_device(): lax.psum((jnp.sum(upstream, axis=0), jnp.sum(upstream * normalized, axis=...  64.2 us
    psum x1, blocking collectives, per_device(): lax.psum(jnp.sum(deviation * deviation, axis=0), ('bx', 'by')) / total_count  62.7 us
    dot_general x2, matrix products, backward_block(): jnp.einsum('kbw,bkc->wc', selector, column_grad, precision=lax.Precision....  57.4 us
    reduce_scatter x1, waiting for transfers between devices, per_device(): lax.psum_scatter(partial_x, 'by', scatter_dimension=2, tiled=True)  27 us
    dot_general x2, matrix products, forward_block(): jnp.einsum('kbw,wc->bkc', selector, window, preferred_element_type=jnp.fl...  25.9 us
    ppermute x4, waiting for transfers between devices, extended(): lax.ppermute(head, axis, [((i + 1) % count, i) for i in range(ends)])  12.1 us
  transfers between devices with their start and end apart: 10, of which 6 were waited for; matrix products, arithmetic and copies ran while one was open for 2% of the time, Pallas kernels for 0%

commit v1 on v0

--- a/solution.py
+++ b/solution.py
@@ -4,6 +4,10 @@
 from jax.sharding import PartitionSpec as P
 
 epsilon = 1e-05
+
+
+def return_all_blocks_for(matrix, along_axis):
+    return jnp.sum(lax.all_gather(matrix, axis_name=along_axis), 0)
 
 
 def extended(cells, sides, width):
@@ -88,7 +92,9 @@
     )
     center = total_sum / total_count
     deviation = (conv_float - center) * live_mask
-    variance = lax.psum(jnp.sum(deviation * deviation, axis=0), ("bx", "by")) / total_count
+    variance = (
+        return_all_blocks_for(jnp.sum(deviation * deviation, axis=0), ("bx", "by")) / total_count
+    )
     inverse_std = lax.rsqrt(variance + epsilon)
     normalized = (conv_float - center) * inverse_std
     before = gain * normalized + shift

time: 466 us -> 433 us (0.929)
  blocking collectives: 197 us -> 163 us
    psum x1 -> x0, blocking collectives: 62.7 us -> none  [per_device(): lax.psum(jnp.sum(deviation * deviation, axis=0), ('bx', 'by')) / total_count]
    all_gather x0 -> x1, blocking collectives: none -> 28.7 us  [return_all_blocks_for(): return jnp.sum(lax.all_gather(matrix, axis_name=along_axis), 0)]
where the time goes in v1:
time: 433 us; the launch traced here: 432 us
  blocking collectives  163 us (38%)
  waiting for transfers between devices  103 us (24%)
  matrix products  99.4 us (23%)
  between operations  16.4 us (4%)
  local copies, waits for them, and re-layouts  15.4 us (4%)
  starting transfers between devices  14.8 us (3%)
  other arithmetic  13.8 us (3%)
  loops' own time  5.44 us (1%)
    psum x1, blocking collectives, per_device(): lax.psum((jnp.sum(conv_float * live_mask, axis=0), local_count), ('bx', '...  70.3 us
    unnamed x3, waiting for transfers between devices  64.7 us
    psum x1, blocking collectives, per_device(): lax.psum((jnp.sum(upstream, axis=0), jnp.sum(upstream * normalized, axis=...  64 us
    dot_general x2, matrix products, backward_block(): jnp.einsum('kbw,bkc->wc', selector, column_grad, precision=lax.Precision....  57.4 us
    all_gather x1, blocking collectives, return_all_blocks_for(): return jnp.sum(lax.all_gather(matrix, axis_name=along_axis), 0)  28.7 us
    reduce_scatter x1, waiting for transfers between devices, per_device(): lax.psum_scatter(partial_x, 'by', scatter_dimension=2, tiled=True)  27 us
    dot_general x2, matrix products, forward_block(): jnp.einsum('kbw,wc->bkc', selector, window, preferred_element_type=jnp.fl...  25.9 us
    ppermute x4, waiting for transfers between devices, extended(): lax.ppermute(head, axis, [((i + 1) % count, i) for i in range(ends)])  11.6 us
  transfers between devices with their start and end apart: 10, of which 6 were waited for; matrix products, arithmetic and copies ran while one was open for 2% of the time, Pallas kernels for 0%

profile of v1, /device:TPU:0, one launch (start us, length us, event | category | flops | bytes accessed | tf_op | source)
XLA Modules:
  0.0 431.7 jit_solution(18226685468647096655)
XLA Ops:
  7.2 1.9 fusion.34
  9.1 3.9 collective-permute-start
  13.0 1.3 collective-permute-start.1
  15.2 4.3 %collective-permute-done.1 = bf16[1,3,128,128]{3,2,1,0:T(8,128)(2,1)S(1)} collective-permute-done((bf16[1,3,128,128]{3,2,1,0:T(8,128)(2,1)S(1)}, bf16[1,3,128,128]{3,2,1,0:T(8,128)(2,1)S(1)}, u32[]{:S(2)}, u32[]{:S(2)}) %collective-permute-start.1) | collective-permute-done | bytes 98336 | tf_op jit(solution)/shard_map/ppermute | solution.py:23
  20.3 1.9 collective-permute-start.2
  22.2 1.3 collective-permute-start.3
  25.5 1.5 collective-permute-done.3
  28.2 38.2 %while.33 = (s32[]{:T(128)}, bf16[2,512,128]{2,1,0:T(8,128)(2,1)S(1)}, bf16[2,512,3456]{1,2,0:T(8,128)(2,1)}, bf16[2,512,128]{2,1,0:T(8,128)(2,1)}, bf16[2,9,64,...) while((s32[]{:T(128)}, ...), condition=%wide.region_1.2_spmd.clone, body=%wide.region_0.1_spmd.sunk.clone | while | flops 4321123840 | bytes 16304801 | solution.py:81
  31.2 13.0 %fusion.82 = bf16[128,27,512]{2,0,1:T(8,128)(2,1)S(1)} fusion(s32[27,512]{1,0:T(8,128)S(1)} %bitcast_select_fusion.6, bf16[576,128]{1,0:T(8,128)(2,1)S(1)} %bitcast.224, bf16[512,128]{1,0:T(8,128)(2,1)S(1)} %dynamic-slice_bitcast_fusion.3), kind=kOutput, calls=%fused_computation.3.clone.1.clone | convolution fusion | flops 3867738112 | bytes 3872768 | tf_op jit(solution)/shard_map/while/body/eval_jaxpr/kbw,wc->bkc/dot_general | solution.py:75
  44.1 2.0 constant_dynamic-update-slice_fusion.6
  46.1 1.2 fusion.83
  50.2 13.0 %fusion.82 = bf16[128,27,512]{2,0,1:T(8,128)(2,1)S(1)} fusion(s32[27,512]{1,0:T(8,128)S(1)} %bitcast_select_fusion.6, bf16[576,128]{1,0:T(8,128)(2,1)S(1)} %bitcast.224, bf16[512,128]{1,0:T(8,128)(2,1)S(1)} %dynamic-slice_bitcast_fusion.3), kind=kOutput, calls=%fused_computation.3.clone.1.clone | convolution fusion | flops 3867738112 | bytes 3872768 | tf_op jit(solution)/shard_map/while/body/eval_jaxpr/kbw,wc->bkc/dot_general | solution.py:75
  63.2 2.0 constant_dynamic-update-slice_fusion.6
  66.6 70.3 %all-reduce.2 = (f32[128]{0:T(128)S(1)}, f32[]{:T(128)}) all-reduce(f32[128]{0:T(128)S(1)} %multiply_reduce_fusion.1, f32[]{:T(128)} %fusion.44), channel_id=1, replica_groups=mesh['bx'=16,'by'=8] {'bx','by'}, use_global_device_ids=true, to_apply=%region_3.4 | all-reduce | flops 129 | bytes 1032 | tf_op jit(solution)/shard_map/psum | solution.py:90
  137.8 28.7 %all-gather.1 = f32[128,1,128]{2,1,0:T(1,128)S(1)} all-gather(f32[1,1,128]{2,1,0:T(1,128)S(1)} %bitcast.241), channel_id=2, replica_groups=mesh['bx'=16,'by'=8] {'bx','by'}, dimensions={0}, use_global_device_ids=true | all-gather | bytes 66048 | tf_op jit(solution)/shard_map/all_gather | solution.py:10
  167.4 1.2 fusion.39
  168.5 64.0 %all-reduce.1 = (f32[128]{0:T(128)S(1)}, f32[128]{0:T(128)S(1)}) all-reduce(f32[128]{0:T(128)S(1)} %get-tuple-element.329, f32[128]{0:T(128)S(1)} %get-tuple-element.328), channel_id=1, replica_groups=mesh['bx'=16,'by'=8] {'bx','by'}, use_global_device_ids=true, to_apply=%region_11.12 | all-reduce | flops 256 | bytes 2048 | tf_op jit(solution)/shard_map/psum | solution.py:103
  232.5 1.9 fusion.42
  234.4 73.1 %while.34 = (s32[]{:T(128)}, f32[3456,128]{1,0:T(8,128)S(1)}, f32[2,512,128]{2,1,0:T(8,128)}, bf16[2,9,64,128]{3,2,0,1:T(8,128)(2,1)}, bf16[2,512,3456]{1,2,0:T(...) while((s32[]{:T(128)}, f32[3456,128]{1,0:T(8,128)S(1)}, ...), condition=%wide.region_13.14_spmd.clone.clone, body=%wide.region_12.13_spmd.clone.sunk.clone | while | flops 24024522752 | bytes 28413672 | solution.py:136
  237.5 28.7 %fusion.90 = f32[1088,128]{1,0:T(8,128)S(1)} fusion(f32[512,27,128]{2,0,1:T(8,128)S(1)} %fusion.89, s32[27,512]{1,0:T(8,128)S(1)} %bitcast_select_fusion.7), kind=kOutput, calls=%fused_computation.31.clone.1.clone | convolution fusion | flops 23117266944 | bytes 7690240 | tf_op jit(solution)/shard_map/while/body/eval_jaxpr/kbw,bkc->wc/dot_general | solution.py:123
  267.8 3.2 convolution_add_fusion.3
  274.1 28.7 %fusion.90 = f32[1088,128]{1,0:T(8,128)S(1)} fusion(f32[512,27,128]{2,0,1:T(8,128)S(1)} %fusion.89, s32[27,512]{1,0:T(8,128)S(1)} %bitcast_select_fusion.7), kind=kOutput, calls=%fused_computation.31.clone.1.clone | convolution fusion | flops 23117266944 | bytes 7690240 | tf_op jit(solution)/shard_map/while/body/eval_jaxpr/kbw,bkc->wc/dot_general | solution.py:123
  304.3 3.2 convolution_add_fusion.3
  309.6 2.4 collective-permute-start.4
  312.0 1.3 collective-permute-start.5
  315.3 3.6 collective-permute-done.5
  319.9 1.4 collective-permute-start.6
  321.2 1.3 collective-permute-start.7
  323.4 2.1 collective-permute-done.7
  326.8 64.7 %all-reduce.5.cloned.1.call-done = bf16[27,128,128]{2,1,0:T(8,128)(2,1)} async-done(((bf16[27,128,128]{2,1,0:T(8,128)(2,1)}), bf16[27,128,128]{2,1,0:T(8,128)(2,1)}) %all-reduce.5.cloned.1.call-update) | async-done | bytes 884752
  393.2 3.2 fusion.35
  396.4 27.0 %reduce-scatter.3.cloned.1.call-done = bf16[27,8,16]{0,1,2:T(8,128)(2,1)} async-done(((bf16[27,8,128]{0,1,2:T(8,128)(2,1)}), bf16[27,8,16]{0,1,2:T(8,128)(2,1)}) %reduce-scatter.3.cloned.1.call-update) | async-done | bytes 6928 | tf_op jit(solution)/shard_map/reduce_scatter | solution.py:143
  (85 shorter events, 25.7 us)
Async XLA Ops:
  7.2 21.0 %copy-start = (bf16[3456,128]{1,0:T(8,128)(2,1)S(1)}, bf16[3456,128]{1,0:T(8,128)(2,1)}, u32[]{:S(2)}) copy-start(bf16[3456,128]{1,0:T(8,128)(2,1)} %param.16) | copy-start | bytes 2654212
  7.2 384.3 %all-reduce.5.cloned.1.call-start = ((), (), s32[]{:S(2)}) async-start(), calls=%async_computation.2 | async-start | bytes 1769472
  9.1 6.1 %collective-permute-start = (bf16[1,3,128,128]{3,2,1,0:T(8,128)(2,1)S(1)}, bf16[1,3,128,128]{3,2,1,0:T(8,128)(2,1)S(1)}, u32[]{:S(2)}, u32[]{:S(2)}) collective-permute-start(bf16[1,3,128,128]{3,2,1,0:T(8,128)(2,1)S(1)} %bitcast.240), channel_id=1, source_target_pairs={{0,8},{8,16},{16,24},{24,32},{32,40},{40,48},{48,56},{56,64},{64,7... | collective-permute-start | bytes 294920 | tf_op jit(solution)/shard_map/ppermute | solution.py:21
  13.0 6.5 %collective-permute-start.1 = (bf16[1,3,128,128]{3,2,1,0:T(8,128)(2,1)S(1)}, bf16[1,3,128,128]{3,2,1,0:T(8,128)(2,1)S(1)}, u32[]{:S(2)}, u32[]{:S(2)}) collective-permute-start(bf16[1,3,128,128]{3,2,1,0:T(8,128)(2,1)S(1)} %bitcast.239), channel_id=1, source_target_pairs={{8,0},{16,8},{24,16},{32,24},{40,32},{48,40},{56,48},{64,56},{72,6... | collective-permute-start | bytes 294920 | tf_op jit(solution)/shard_map/ppermute | solution.py:23
  20.3 5.2 %collective-permute-start.2 = (bf16[5,1,128,128]{3,2,1,0:T(8,128)(2,1)}, bf16[5,1,128,128]{3,2,1,0:T(8,128)(2,1)}, u32[]{:S(2)}, u32[]{:S(2)}) collective-permute-start(bf16[5,1,128,128]{3,2,1,0:T(8,128)(2,1)} %get-tuple-element.372), channel_id=1, source_target_pairs={{0,1},{1,2},{2,3},{3,4},{4,5},{5,6},{6,7},{8,9},{9,10},{10,11},{11... | collective-permute-start | bytes 491528 | tf_op jit(solution)/shard_map/ppermute | solution.py:21
  22.2 4.8 %collective-permute-start.3 = (bf16[5,1,128,128]{3,2,1,0:T(8,128)(2,1)}, bf16[5,1,128,128]{3,2,1,0:T(8,128)(2,1)}, u32[]{:S(2)}, u32[]{:S(2)}) collective-permute-start(bf16[5,1,128,128]{3,2,1,0:T(8,128)(2,1)} %get-tuple-element.373), channel_id=1, source_target_pairs={{1,0},{2,1},{3,2},{4,3},{5,4},{6,5},{7,6},{9,8},{10,9},{11,10},{12... | collective-permute-start | bytes 491528 | tf_op jit(solution)/shard_map/ppermute | solution.py:23
  28.2 138.5 %copy-start.1 = (f32[128]{0:T(128)S(1)}, f32[128]{0:T(128)}, u32[]{:S(2)}) copy-start(f32[128]{0:T(128)} %param.17) | copy-start | bytes 1540
  28.2 139.1 %copy-start.2 = (f32[128]{0:T(128)S(1)}, f32[128]{0:T(128)}, u32[]{:S(2)}) copy-start(f32[128]{0:T(128)} %param.18) | copy-start | bytes 1540
  234.4 78.9 %copy-start.6 = (u32[128]{0:T(128)S(1)}, u32[128]{0:T(128)}, u32[]{:S(2)}) copy-start(u32[128]{0:T(128)} %constant.182) | copy-start | bytes 1540
  237.5 28.7 %copy-start.3 = (f32[2,512,128]{2,1,0:T(8,128)S(1)}, f32[2,512,128]{2,1,0:T(8,128)}, u32[]{:S(2)}) copy-start(f32[2,512,128]{2,1,0:T(8,128)} %get-tuple-element.580) | copy-start | bytes 1572868 | tf_op jit(solution)/shard_map/while
  266.3 0.8 copy-start.4
  274.1 28.7 %copy-start.3 = (f32[2,512,128]{2,1,0:T(8,128)S(1)}, f32[2,512,128]{2,1,0:T(8,128)}, u32[]{:S(2)}) copy-start(f32[2,512,128]{2,1,0:T(8,128)} %get-tuple-element.580) | copy-start | bytes 1572868 | tf_op jit(solution)/shard_map/while
  302.8 0.8 copy-start.4
  307.6 85.7 %copy-start.5 = (s32[1,1,8,128]{3,2,1,0:T(8,128)S(1)}, s32[1,1,8,128]{3,2,1,0:T(8,128)}, u32[]{:S(2)}) copy-start(s32[1,1,8,128]{3,2,1,0:T(8,128)} %param.15) | copy-start | bytes 12292
  308.6 114.8 %reduce-scatter.3.cloned.1.call-start = ((), (), s32[]{:S(2)}) async-start(), calls=%async_computation.1 | async-start | bytes 294912 | tf_op jit(solution)/shard_map/reduce_scatter | solution.py:143
  309.6 5.6 %collective-permute-start.4 = (bf16[1,3,128,128]{3,2,1,0:T(8,128)(2,1)S(1)}, bf16[1,3,128,128]{3,2,1,0:T(8,128)(2,1)S(1)}, u32[]{:S(2)}, u32[]{:S(2)}) collective-permute-start(bf16[1,3,128,128]{3,2,1,0:T(8,128)(2,1)S(1)} %bitcast.238), channel_id=1, source_target_pairs={{0,8},{8,16},{16,24},{24,32},{32,40},{40,48},{48,56},{56,64},{64,7... | collective-permute-start | bytes 294920 | tf_op jit(solution)/shard_map/ppermute | solution.py:21
  312.0 6.9 %collective-permute-start.5 = (bf16[1,3,128,128]{3,2,1,0:T(8,128)(2,1)S(1)}, bf16[1,3,128,128]{3,2,1,0:T(8,128)(2,1)S(1)}, u32[]{:S(2)}, u32[]{:S(2)}) collective-permute-start(bf16[1,3,128,128]{3,2,1,0:T(8,128)(2,1)S(1)} %bitcast.237), channel_id=1, source_target_pairs={{8,0},{16,8},{24,16},{32,24},{40,32},{48,40},{56,48},{64,56},{72,6... | collective-permute-start | bytes 294920 | tf_op jit(solution)/shard_map/ppermute | solution.py:23
  319.9 3.6 collective-permute-start.6
  321.2 4.4 %collective-permute-start.7 = (bf16[5,1,128,128]{3,2,1,0:T(8,128)(2,1)S(1)}, bf16[5,1,128,128]{3,2,1,0:T(8,128)(2,1)S(1)}, u32[]{:S(2)}, u32[]{:S(2)}) collective-permute-start(bf16[5,1,128,128]{3,2,1,0:T(8,128)(2,1)S(1)} %get-tuple-element.371), channel_id=1, source_target_pairs={{1,0},{2,1},{3,2},{4,3},{5,4},{6,5},{7,6},{9,8},{10,9},{11,10},{12... | collective-permute-start | bytes 491528 | tf_op jit(solution)/shard_map/ppermute | solution.py:23
Sparse Core Ops, SparseCore 0:
  308.8 82.6 all-reduce.4
  393.8 29.5 reduce-scatter.2
